TPU v7x, 32 devices: a whole 2x2x4 slice. The times are simulated.
32 devices in a mesh: perm: 2 (over y), subj: 8 (over z, core), vert: 2 (over x).
Axes of the slice: x: 2, y: 2, z: 4, core: 2. Of those that a mesh axis runs over, the one named last changes fastest.
Arguments:
- kinship: bfloat16 [2048, 2048], P('subj')
- phenotype: bfloat16 [2048, 2048], P('subj', 'vert')
- shuffle: int32 [4096], P(('perm', 'subj')), parts along dimension 0, may hold values from 0 to 2047, as said below
Outputs:
- statistic: float32 [4096], P(('perm', 'vert')), parts along dimension 0
There are 2 independent parts, one for each index of `perm`. A program takes and returns all parts, laid end to end along the dimension named above; an argument that names none is the same for every part. Nothing has to cross between parts.
Inputs may be any that keep to these rules, and one draw needn't show every extreme that they name: shuffle is a permutation of 0 to 2047 that maps every subject into its own exchangeability block.
All inputs are finite; a program needn't handle non-finite values.
Results may differ from a plain program's by a relative error of at most 0.0003.
Values may be sent and summed in bfloat16 or wider, within the bound.
A program may use at most 128 MiB of HBM per device.

v0:
```python
import jax
import jax.numpy as jnp
from jax import lax
from jax.sharding import PartitionSpec as P


def per_device(kinship, phenotype, shuffle):
    row_count = phenotype.shape[0]
    subject_count = kinship.shape[1]
    row_offset = lax.axis_index("subj") * row_count
    shuffle_all = lax.all_gather(shuffle, "subj", axis=0, tiled=True)
    own_block = lax.dynamic_slice_in_dim(kinship, row_offset, row_count, 1)
    kin_diag = jnp.diagonal(own_block).astype(jnp.float32)
    inverse = (
        jnp.zeros((subject_count,), jnp.int32)
        .at[shuffle_all]
        .set(jnp.arange(subject_count, dtype=jnp.int32))
    )
    kin_moved = jnp.take(kinship, inverse, axis=1)
    piece = lax.all_gather(phenotype, "subj", axis=0, tiled=True)
    piece_rows = piece.shape[0]
    targets = jnp.arange(piece_rows, dtype=jnp.int32)
    picker = (shuffle[:, None] == targets[None, :]).astype(jnp.bfloat16)
    product = jnp.dot(kin_moved, piece, preferred_element_type=jnp.float32)
    picked = jnp.dot(picker, piece, preferred_element_type=jnp.float32)
    local_perm = picked.astype(jnp.bfloat16)
    moved = local_perm.astype(jnp.float32)
    cross_term = jnp.sum(moved * (product - kin_diag[:, None] * moved), axis=0)
    values = phenotype.astype(jnp.float32)
    squares = jnp.sum(values * values, axis=0)
    cross_all, squares_all = lax.psum((cross_term, squares), "subj")
    return cross_all / (
        jnp.sqrt(jnp.float32(subject_count)) * (squares_all / subject_count + 1e-05)
    )


def solution(mesh):
    in_specs = (P("subj", None), P("subj", "vert"), P(("perm", "subj")))
    out_specs = P(("perm", "vert"))
    return jax.shard_map(
        per_device, mesh=mesh, in_specs=in_specs, out_specs=out_specs, check_vma=False
    )
```

profile of v0, /device:TPU:0, one launch (start us, length us, event | category | flops | bytes accessed | tf_op | source)
XLA Modules:
  0.0 86.2 jit_solution(4435707539312031258)
XLA Ops:
  6.5 0.0 all-gather.3.cloned.1.call-start
  6.5 0.7 all-gather.3.cloned.1.call-update
  7.3 1.5 %copy.6 = bf16[256,2048]{0,1:T(8,128)(2,1)S(1)} copy(bf16[256,2048]{1,0:T(8,128)(2,1)} %param.3) | data formatting | bytes 2097152 | tf_op args[0]
  8.8 0.9 %constant_dynamic-slice_fusion = bf16[256,256]{1,0:T(8,128)(2,1)S(1)} fusion(bf16[256,2048]{1,0:T(8,128)(2,1)} %param.3, s32[]{:T(128)S(6)} %select_n.22), kind=kLoop, calls=%fused_computation.23 | loop fusion | bytes 262148 | tf_op jit(solution)/shard_map/dynamic_slice | solution.py:12
  9.7 2.5 %gather_fusion.1 = bf16[256]{0:T(256)(128)(2,1)S(1)} fusion(bf16[256,256]{1,0:T(8,128)(2,1)S(1)} %constant_dynamic-slice_fusion, s32[256]{0:T(256)S(1)} %bitcast.5), kind=kCustom, calls=%fused_computation.1 | custom fusion | bytes 3072 | tf_op jit(solution)/shard_map/jit(diagonal)/cond/branch_0_fun/gather | solution.py:13
  12.2 13.7 %all-gather = s32[8,1,256]{2,1,0:T(1,128)S(1)} all-gather(s32[1,1,256]{2,1,0:T(1,128)} %bitcast.7), channel_id=1, replica_groups=mesh['perm'=2,'subj'=8,'vert'=2] {'subj'}, dimensions={0}, use_global_device_ids=true | all-gather | bytes 9216 | tf_op jit(solution)/shard_map/all_gather | solution.py:11
  26.0 8.0 %scatter_custom_fusion = s32[2048]{0:T(1024)S(1)} fusion(s32[2048]{0:T(1024)S(1)} %compare_select_fusion.1, s32[2048]{0:T(1024)S(1)} %iota.16, s32[]{:T(128)} %constant.12.clone.1), kind=kCustom, calls=%fused_computation.20 | custom fusion | bytes 8196 | tf_op jit(solution)/shard_map/scatter | solution.py:17
  34.0 0.0 copy-start
  34.0 0.0 copy-start.1
  34.0 7.5 %gather_fusion = bf16[2048,256]{1,0:T(8,128)(2,1)S(1)} fusion(bf16[256,2048]{0,1:T(8,128)(2,1)S(1)} %copy.6, s32[2048]{0:T(1024)S(1)} %fusion.7), kind=kCustom, calls=%fused_computation | custom fusion | bytes 2105344 | tf_op jit(solution)/shard_map/jit(_take)/gather | solution.py:19
  41.5 0.0 copy-done
  41.6 0.1 multiply_reduce_fusion
  41.7 16.9 %all-gather.3.cloned.1.call-done = bf16[2048,1024]{1,0:T(8,128)(2,1)} async-done(((bf16[256,1024]{1,0:T(8,128)(2,1)}), bf16[2048,1024]{1,0:T(8,128)(2,1)}) %all-gather.3.cloned.1.call-update) | async-done | bytes 4194320 | tf_op jit(solution)/shard_map/all_gather | solution.py:20
  58.6 0.0 copy-done.1
  58.6 0.0 copy-start.2
  58.6 3.6 %fusion.1 = bf16[256,1024]{1,0:T(8,128)(2,1)S(1)} fusion(bf16[2048,1024]{1,0:T(8,128)(2,1)} %all-gather.3.cloned.1.call-done, s32[256]{0:T(256)S(1)} %copy-done.1), kind=kOutput, calls=%fused_computation.8 | convolution fusion | flops 1074528256 | bytes 4719616 | tf_op jit(solution)/shard_map/dot_general | solution.py:25
  62.2 0.0 copy-done.2
  62.2 1.5 %fusion.2 = f32[1024]{0:T(1024)S(1)} fusion(bf16[2048,1024]{1,0:T(8,128)(2,1)S(1)} %copy-done.2, bf16[256,1024]{1,0:T(8,128)(2,1)S(1)} %fusion.1, bf16[2048,256]{1,0:T(8,128)(2,1)S(1)} %gather_fusion, pred[2048]{0:T(1024)(128)(4,1)S(1)} %compare_and_fusion, f32[256]{0:T(256)S(1)} %convert_element_type.19), kind=kOutput, calls=%fused_computation.9 | convolution fusion | flops 1075575808 | bytes 5774336 | tf_op jit(solution)/shard_map/dot_general | solution.py:24
  63.7 15.1 %all-reduce = (f32[1024]{0:T(1024)S(1)}, f32[1024]{0:T(1024)S(1)}) all-reduce(f32[1024]{0:T(1024)S(1)} %fusion.2, f32[1024]{0:T(1024)S(1)} %multiply_reduce_fusion), channel_id=1, replica_groups=mesh['perm'=2,'subj'=8,'vert'=2] {'subj'}, use_global_device_ids=true, to_apply=%region_2.3 | all-reduce | flops 2048 | bytes 16384 | tf_op jit(solution)/shard_map/psum | solution.py:31
  78.8 0.6 multiply_divide_fusion
  (6 shorter events, 0.0 us)
Async XLA Ops:
  6.5 52.0 %all-gather.3.cloned.1.call-start = ((), (), s32[]{:S(2)}) async-start(), calls=%async_computation | async-start | bytes 4718592 | tf_op jit(solution)/shard_map/all_gather | solution.py:20
  34.0 7.5 %copy-start = (bf16[256,1024]{1,0:T(8,128)(2,1)S(1)}, bf16[256,1024]{1,0:T(8,128)(2,1)}, u32[]{:S(2)}) copy-start(bf16[256,1024]{1,0:T(8,128)(2,1)} %param.4) | copy-start | bytes 1572868
  34.0 24.5 %copy-start.1 = (s32[256]{0:T(256)S(1)}, s32[256]{0:T(256)}, u32[]{:S(2)}) copy-start(s32[256]{0:T(256)} %param.5) | copy-start | bytes 3076
  58.6 3.6 %copy-start.2 = (bf16[2048,1024]{1,0:T(8,128)(2,1)S(1)}, bf16[2048,1024]{1,0:T(8,128)(2,1)}, u32[]{:S(2)}) copy-start(bf16[2048,1024]{1,0:T(8,128)(2,1)} %all-gather.3.cloned.1.call-done) | copy-start | bytes 12582916
Sparse Core Ops, SparseCore 0:
  8.9 49.5 all-gather.2
where the time goes:
time: 86.4 us; the launch traced here: 86.2 us
  blocking collectives  28.8 us (33%)
  local copies, waits for them, and re-layouts  20.5 us (24%)
  waiting for transfers between devices  17.6 us (20%)
  between operations  13.5 us (16%)
  matrix products  5.08 us (6%)
    all_gather x1, waiting for transfers between devices, per_device(): piece = lax.all_gather(phenotype, 'subj', axis=0, tiled=True)  16.9 us
    psum x1, blocking collectives, per_device(): cross_all, squares_all = lax.psum((cross_term, squares), 'subj')  15.1 us
    all_gather x1, blocking collectives, per_device(): shuffle_all = lax.all_gather(shuffle, 'subj', axis=0, tiled=True)  13.7 us
    scatter x1, local copies, waits for them, and re-layouts, per_device(): inverse = jnp.zeros((subject_count,), jnp.int32).at[shuffle_all].set(jnp....  8.05 us
    gather x1, local copies, waits for them, and re-layouts, per_device(): kin_moved = jnp.take(kinship, inverse, axis=1)  7.5 us
    dot_general x1, matrix products, per_device(): picked = jnp.dot(picker, piece, preferred_element_type=jnp.float32)  3.62 us
    gather x1, local copies, waits for them, and re-layouts, per_device(): kin_diag = jnp.diagonal(own_block).astype(jnp.float32)  2.49 us
  transfers between devices with their start and end apart: 1, of which 1 were waited for; matrix products, arithmetic and copies ran while one was open for 24% of the time, Pallas kernels for 0%

commit v1 on v0

--- a/solution.py
+++ b/solution.py
@@ -17,7 +17,12 @@
         .set(jnp.arange(subject_count, dtype=jnp.int32))
     )
     kin_moved = jnp.take(kinship, inverse, axis=1)
-    piece = lax.all_gather(phenotype, "subj", axis=0, tiled=True)
+    ring = [phenotype]
+    for hop in range(7):
+        ring.append(lax.ppermute(ring[-1], "subj", [(dev, (dev + 1) % 8) for dev in range(8)]))
+    piece = jnp.roll(
+        jnp.concatenate(ring[::-1], axis=0), (lax.axis_index("subj") + 1) * ring[0].shape[0], axis=0
+    )
     piece_rows = piece.shape[0]
     targets = jnp.arange(piece_rows, dtype=jnp.int32)
     picker = (shuffle[:, None] == targets[None, :]).astype(jnp.bfloat16)

time: 86.4 us -> 116 us (1.34)
  waiting for transfers between devices: 17.6 us -> 54.3 us
  between operations: 13.5 us -> 0.23 us
  local copies, waits for them, and re-layouts: 20.5 us -> 30.7 us
  blocking collectives: 28.8 us -> 26.3 us
  matrix products: 5.08 us -> 2.79 us
    ppermute x0 -> x7, waiting for transfers between devices: none -> 54.3 us  [per_device(): lax.ppermute(ring[-1], 'subj', [(dev, (dev + 1) % 8) for dev in range(8)])]
    all_gather x1 -> x0, waiting for transfers between devices: 16.9 us -> none  [per_device(): piece = lax.all_gather(phenotype, 'subj', axis=0, tiled=True)]
    unnamed x7 -> x26, local copies, waits for them, and re-layouts: 1.5 us -> 10.2 us
    all_gather x1, blocking collectives: 13.7 us -> 10.4 us  [per_device(): shuffle_all = lax.all_gather(shuffle, 'subj', axis=0, tiled=True)]
    dot_general x1, matrix products: 3.62 us -> 1.34 us  [per_device(): picked = jnp.dot(picker, piece, preferred_element_type=jnp.float32)]
    gather x1, local copies, waits for them, and re-layouts: 7.5 us -> 9.02 us  [per_device(): kin_moved = jnp.take(kinship, inverse, axis=1)]
  transfers between devices with their start and end apart: 1 -> 7, of which waited for: 1 -> 6; matrix products, arithmetic and copies ran while one was open for 24% -> 19% of each run, Pallas kernels for 0% -> 0%
where the time goes in v1:
time: 116 us
  waiting for transfers between devices  54.3 us (47%)
  local copies, waits for them, and re-layouts  30.7 us (26%)
  blocking collectives  26.3 us (23%)
  matrix products  2.79 us (2%)
    ppermute x7, waiting for transfers between devices, per_device(): lax.ppermute(ring[-1], 'subj', [(dev, (dev + 1) % 8) for dev in range(8)])  54.3 us
    psum x1, blocking collectives, per_device(): cross_all, squares_all = lax.psum((cross_term, squares), 'subj')  15.9 us
    all_gather x1, blocking collectives, per_device(): shuffle_all = lax.all_gather(shuffle, 'subj', axis=0, tiled=True)  10.4 us
    unnamed x26, local copies, waits for them, and re-layouts  10.2 us
    gather x1, local copies, waits for them, and re-layouts, per_device(): kin_moved = jnp.take(kinship, inverse, axis=1)  9.02 us
    scatter x1, local copies, waits for them, and re-layouts, per_device(): inverse = jnp.zeros((subject_count,), jnp.int32).at[shuffle_all].set(jnp....  8.05 us
    gather x1, local copies, waits for them, and re-layouts, per_device(): kin_diag = jnp.diagonal(own_block).astype(jnp.float32)  2.49 us
  transfers between devices with their start and end apart: 7, of which 6 were waited for; matrix products, arithmetic and copies ran while one was open for 19% of the time, Pallas kernels for 0%

profile of v1, /device:TPU:0, one launch (start us, length us, event | category | flops | bytes accessed | tf_op | source)
XLA Modules:
  0.0 115.7 jit_solution(15502428397874545253)
XLA Ops:
  0.0 0.5 collective-permute-start
  0.5 11.2 %collective-permute-done = bf16[256,1024]{1,0:T(8,128)(2,1)S(1)} collective-permute-done((bf16[256,1024]{1,0:T(8,128)(2,1)}, bf16[256,1024]{1,0:T(8,128)(2,1)S(1)}, u32[]{:S(2)}, u32[]{:S(2)}) %collective-permute-start) | collective-permute-done | bytes 524320 | tf_op jit(solution)/shard_map/ppermute | solution.py:22
  11.7 0.0 collective-permute-start.1
  11.7 10.4 %collective-permute-done.1 = bf16[256,1024]{1,0:T(8,128)(2,1)S(1)} collective-permute-done((bf16[256,1024]{1,0:T(8,128)(2,1)S(1)}, bf16[256,1024]{1,0:T(8,128)(2,1)S(1)}, u32[]{:S(2)}, u32[]{:S(2)}) %collective-permute-start.1) | collective-permute-done | bytes 524320 | tf_op jit(solution)/shard_map/ppermute | solution.py:22
  22.1 0.0 collective-permute-start.2
  22.1 10.4 %collective-permute-done.2 = bf16[256,1024]{1,0:T(8,128)(2,1)S(1)} collective-permute-done((bf16[256,1024]{1,0:T(8,128)(2,1)S(1)}, bf16[256,1024]{1,0:T(8,128)(2,1)S(1)}, u32[]{:S(2)}, u32[]{:S(2)}) %collective-permute-start.2) | collective-permute-done | bytes 524320 | tf_op jit(solution)/shard_map/ppermute | solution.py:22
  32.5 0.0 collective-permute-start.3
  32.5 10.4 %collective-permute-done.3 = bf16[256,1024]{1,0:T(8,128)(2,1)S(1)} collective-permute-done((bf16[256,1024]{1,0:T(8,128)(2,1)S(1)}, bf16[256,1024]{1,0:T(8,128)(2,1)S(1)}, u32[]{:S(2)}, u32[]{:S(2)}) %collective-permute-start.3) | collective-permute-done | bytes 524320 | tf_op jit(solution)/shard_map/ppermute | solution.py:22
  42.9 0.8 copy-done.1
  43.7 0.0 collective-permute-start.4
  43.7 10.5 %collective-permute-done.4 = bf16[256,1024]{1,0:T(8,128)(2,1)} collective-permute-done((bf16[256,1024]{1,0:T(8,128)(2,1)S(1)}, bf16[256,1024]{1,0:T(8,128)(2,1)}, u32[]{:S(2)}, u32[]{:S(2)}) %collective-permute-start.4) | collective-permute-done | bytes 524320 | tf_op jit(solution)/shard_map/ppermute | solution.py:22
  54.2 1.5 %copy.6 = bf16[256,2048]{0,1:T(8,128)(2,1)S(1)} copy(bf16[256,2048]{1,0:T(8,128)(2,1)} %param.3) | data formatting | bytes 2097152 | tf_op args[0]
  55.7 0.9 constant_dynamic-slice_fusion
  56.6 2.5 %gather_fusion.1 = bf16[256]{0:T(256)(128)(2,1)S(1)} fusion(bf16[256,256]{1,0:T(8,128)(2,1)S(1)} %constant_dynamic-slice_fusion, s32[256]{0:T(256)S(1)} %bitcast.3), kind=kCustom, calls=%fused_computation.1 | custom fusion | bytes 3072 | tf_op jit(solution)/shard_map/jit(diagonal)/cond/branch_0_fun/gather | solution.py:13
  59.1 10.4 %all-gather = s32[8,1,256]{2,1,0:T(1,128)S(1)} all-gather(s32[1,1,256]{2,1,0:T(1,128)} %bitcast.5), channel_id=1, replica_groups=mesh['perm'=2,'subj'=8,'vert'=2] {'subj'}, dimensions={0}, use_global_device_ids=true | all-gather | bytes 9216 | tf_op jit(solution)/shard_map/all_gather | solution.py:11
  69.5 8.0 %scatter_custom_fusion = s32[2048]{0:T(1024)S(1)} fusion(s32[2048]{0:T(1024)S(1)} %compare_select_fusion.1, s32[2048]{0:T(1024)S(1)} %iota.16, s32[]{:T(128)} %constant.55.clone.1), kind=kCustom, calls=%fused_computation.39 | custom fusion | bytes 8196 | tf_op jit(solution)/shard_map/scatter | solution.py:17
  77.6 0.2 collective-permute-start.6
  77.8 9.0 %gather_fusion = bf16[2048,256]{1,0:T(8,128)(2,1)} fusion(bf16[256,2048]{0,1:T(8,128)(2,1)S(1)} %copy.6, s32[2048]{0:T(1024)S(1)} %fusion.19), kind=kCustom, calls=%fused_computation | custom fusion | bytes 2105344 | tf_op jit(solution)/shard_map/jit(_take)/gather | solution.py:19
  86.8 0.1 multiply_reduce_fusion
  87.0 0.0 copy-start.4
  87.0 1.4 %collective-permute-done.6 = bf16[256,1024]{1,0:T(8,128)(2,1)} collective-permute-done((bf16[256,1024]{1,0:T(8,128)(2,1)}, bf16[256,1024]{1,0:T(8,128)(2,1)}, u32[]{:S(2)}, u32[]{:S(2)}) %collective-permute-start.6) | collective-permute-done | bytes 524320 | tf_op jit(solution)/shard_map/ppermute | solution.py:22
  88.4 1.1 constant_dynamic-update-slice_fusion.15
  89.4 1.1 constant_dynamic-update-slice_fusion.14
  90.5 1.1 constant_dynamic-update-slice_fusion.13
  91.6 1.1 constant_dynamic-update-slice_fusion.12
  92.9 1.2 constant_dynamic-update-slice_fusion.7
  94.0 1.1 constant_dynamic-update-slice_fusion.6
  95.1 1.1 constant_dynamic-update-slice_fusion.5
  96.4 1.3 %fusion.9 = bf16[256,1024]{1,0:T(8,128)(2,1)S(1)} fusion(bf16[4096,1024]{1,0:T(8,128)(2,1)S(1)} %constant_dynamic-update-slice_fusion, s32[]{:T(128)S(6)} %select_n.33, s32[256]{0:T(256)S(1)} %copy-done.4), kind=kOutput, calls=%fused_computation.11 | convolution fusion | flops 1074528256 | bytes 4719620 | tf_op jit(solution)/shard_map/dot_general | solution.py:30
  97.8 1.4 %fusion.12 = f32[1024]{0:T(1024)S(1)} fusion(bf16[4096,1024]{1,0:T(8,128)(2,1)S(1)} %constant_dynamic-update-slice_fusion, s32[]{:T(128)S(6)} %select_n.33, bf16[256,1024]{1,0:T(8,128)(2,1)S(1)} %fusion.9, bf16[2048,256]{1,0:T(8,128)(2,1)S(1)} %copy-done.3, pred[2048]{0:T(1024)(128)(4,1)S(1)} %compare_and_fusion, f32[256]{0:T(256)S(1)} %convert_element_type.19), kind=kOutput, calls=%fused_computation.12 | convolution fusion | flops 1075575808 | bytes 5774340 | tf_op jit(solution)/shard_map/dot_general | solution.py:29
  99.2 15.9 %all-reduce = (f32[1024]{0:T(1024)S(1)}, f32[1024]{0:T(1024)S(1)}) all-reduce(f32[1024]{0:T(1024)S(1)} %fusion.12, f32[1024]{0:T(1024)S(1)} %multiply_reduce_fusion), channel_id=1, replica_groups=mesh['perm'=2,'subj'=8,'vert'=2] {'subj'}, use_global_device_ids=true, to_apply=%region_2.3 | all-reduce | flops 2048 | bytes 16384 | tf_op jit(solution)/shard_map/psum | solution.py:36
  115.1 0.6 multiply_divide_fusion
  (25 shorter events, 0.4 us)
Async XLA Ops:
  0.0 86.8 %copy-start = (bf16[256,1024]{1,0:T(8,128)(2,1)S(1)}, bf16[256,1024]{1,0:T(8,128)(2,1)}, u32[]{:S(2)}) copy-start(bf16[256,1024]{1,0:T(8,128)(2,1)} %param.4) | copy-start | bytes 1572868
  0.0 11.7 %collective-permute-start = (bf16[256,1024]{1,0:T(8,128)(2,1)}, bf16[256,1024]{1,0:T(8,128)(2,1)S(1)}, u32[]{:S(2)}, u32[]{:S(2)}) collective-permute-start(bf16[256,1024]{1,0:T(8,128)(2,1)} %param.4), channel_id=1, source_target_pairs={{0,2},{2,4},{4,6},{6,8},{8,10},{10,12},{12,14},{14,0},{1,3},{3,5},... | collective-permute-start | bytes 1572872 | tf_op jit(solution)/shard_map/ppermute | solution.py:22
  11.7 10.4 %collective-permute-start.1 = (bf16[256,1024]{1,0:T(8,128)(2,1)S(1)}, bf16[256,1024]{1,0:T(8,128)(2,1)S(1)}, u32[]{:S(2)}, u32[]{:S(2)}) collective-permute-start(bf16[256,1024]{1,0:T(8,128)(2,1)S(1)} %collective-permute-done), channel_id=1, source_target_pairs={{0,2},{2,4},{4,6},{6,8},{8,10},{10,12},{12,14},{14,0},{1,3},{3,5},... | collective-permute-start | bytes 1572872 | tf_op jit(solution)/shard_map/ppermute | solution.py:22
  22.1 10.4 %collective-permute-start.2 = (bf16[256,1024]{1,0:T(8,128)(2,1)S(1)}, bf16[256,1024]{1,0:T(8,128)(2,1)S(1)}, u32[]{:S(2)}, u32[]{:S(2)}) collective-permute-start(bf16[256,1024]{1,0:T(8,128)(2,1)S(1)} %collective-permute-done.1), channel_id=1, source_target_pairs={{0,2},{2,4},{4,6},{6,8},{8,10},{10,12},{12,14},{14,0},{1,3},{3,5},... | collective-permute-start | bytes 1572872 | tf_op jit(solution)/shard_map/ppermute | solution.py:22
  32.5 10.4 %collective-permute-start.3 = (bf16[256,1024]{1,0:T(8,128)(2,1)S(1)}, bf16[256,1024]{1,0:T(8,128)(2,1)S(1)}, u32[]{:S(2)}, u32[]{:S(2)}) collective-permute-start(bf16[256,1024]{1,0:T(8,128)(2,1)S(1)} %collective-permute-done.2), channel_id=1, source_target_pairs={{0,2},{2,4},{4,6},{6,8},{8,10},{10,12},{12,14},{14,0},{1,3},{3,5},... | collective-permute-start | bytes 1572872 | tf_op jit(solution)/shard_map/ppermute | solution.py:22
  42.9 0.8 copy-start.1
  43.7 10.5 %collective-permute-start.4 = (bf16[256,1024]{1,0:T(8,128)(2,1)S(1)}, bf16[256,1024]{1,0:T(8,128)(2,1)}, u32[]{:S(2)}, u32[]{:S(2)}) collective-permute-start(bf16[256,1024]{1,0:T(8,128)(2,1)S(1)} %collective-permute-done.3), channel_id=1, source_target_pairs={{0,2},{2,4},{4,6},{6,8},{8,10},{10,12},{12,14},{14,0},{1,3},{3,5},... | collective-permute-start | bytes 1572872 | tf_op jit(solution)/shard_map/ppermute | solution.py:22
  54.2 23.4 %collective-permute-start.5 = (bf16[256,1024]{1,0:T(8,128)(2,1)}, bf16[256,1024]{1,0:T(8,128)(2,1)}, u32[]{:S(2)}, u32[]{:S(2)}) collective-permute-start(bf16[256,1024]{1,0:T(8,128)(2,1)} %collective-permute-done.4), channel_id=1, source_target_pairs={{0,2},{2,4},{4,6},{6,8},{8,10},{10,12},{12,14},{14,0},{1,3},{3,5},... | collective-permute-start | bytes 1572872 | tf_op jit(solution)/shard_map/ppermute | solution.py:22
  77.6 10.8 %collective-permute-start.6 = (bf16[256,1024]{1,0:T(8,128)(2,1)}, bf16[256,1024]{1,0:T(8,128)(2,1)}, u32[]{:S(2)}, u32[]{:S(2)}) collective-permute-start(bf16[256,1024]{1,0:T(8,128)(2,1)} %collective-permute-done.5), channel_id=1, source_target_pairs={{0,2},{2,4},{4,6},{6,8},{8,10},{10,12},{12,14},{14,0},{1,3},{3,5},... | collective-permute-start | bytes 1572872 | tf_op jit(solution)/shard_map/ppermute | solution.py:22
  86.8 9.4 %copy-start.2 = (bf16[256,1024]{1,0:T(8,128)(2,1)S(1)}, bf16[256,1024]{1,0:T(8,128)(2,1)}, u32[]{:S(2)}) copy-start(bf16[256,1024]{1,0:T(8,128)(2,1)} %copy-done.1) | copy-start | bytes 1572868
  87.0 9.4 %copy-start.4 = (s32[256]{0:T(256)S(1)}, s32[256]{0:T(256)}, u32[]{:S(2)}) copy-start(s32[256]{0:T(256)} %param.5) | copy-start | bytes 3076
  92.8 5.0 %copy-start.3 = (bf16[2048,256]{1,0:T(8,128)(2,1)S(1)}, bf16[2048,256]{1,0:T(8,128)(2,1)}, u32[]{:S(2)}) copy-start(bf16[2048,256]{1,0:T(8,128)(2,1)} %gather_fusion) | copy-start | bytes 3145732
